TPU v7x, 128 devices: a whole 4x4x4 slice. The times are simulated.
128 devices in a mesh: lev: 8 (over x, z_lo), mem: 16 (over z_hi, y, core).
Axes of the slice: x: 4, y: 4, z: 4 (z_hi: 2, z_lo: 2; z = z_hi * 2 + z_lo), core: 2. Of those that a mesh axis runs over, the one named last changes fastest.
Arguments:
- control: float32 [4096, 128, 128], P(None, 'mem', 'lev'), may hold values from -6 to 6
- perturb: bfloat16 [4096, 128, 5, 128], P('lev', 'mem'), may hold values from -6 to 6
- member_weights: float32 [128], P('mem'), may hold values from 0.25 to 4
- blocks: bfloat16 [64, 16, 64, 64], P(None, 'mem'), may hold values from -0.1875 to 0.1875
- block_cols: int32 [64, 16], replicated, may hold values from 0 to 63, as said below
- vertical: float32 [128, 128], replicated, may hold values from -4 to 4
Outputs:
- increment: float32 [4096, 5, 128], P(('lev', 'mem'))
Inputs may be any that keep to these rules, and one draw needn't show every extreme that they name: Within a block row the 16 block columns are distinct, and for every j the column block_cols[:, j] names each of the 64 block rows exactly once.
All inputs are finite; a program needn't handle non-finite values.
Results may differ from a plain program's by a relative error of at most 0.0003.
Values may be sent and summed in bfloat16 or wider, within the bound.
No kernel may reach another device: no remote copies, remote signals or barrier semaphores. Data moves between devices by JAX's collectives and lax.ppermute only.
A program may use at most 192 MiB of HBM per device.

v0:
```python
import math
import jax
import jax.numpy as jnp
from jax import lax
from jax.sharding import PartitionSpec as P


def shards(control, perturb, member_weights, blocks, block_cols, vertical):
    nodes_all, mem_dev, lev_dev = control.shape
    num_blocks, stored_count = block_cols.shape
    block_size = nodes_all // num_blocks
    columns = mem_dev * lev_dev
    source = control.reshape(num_blocks, block_size, columns)
    row_numbers = jnp.broadcast_to(
        jnp.arange(num_blocks, dtype=jnp.int32)[:, None], block_cols.shape
    )
    stored_numbers = jnp.arange(stored_count, dtype=jnp.int32)[None, :]
    inverse = jnp.zeros_like(block_cols).at[block_cols, stored_numbers].set(row_numbers)
    empty = jnp.zeros((num_blocks, block_size, columns), jnp.float32)
    summed = empty
    shard_piece = lax.all_gather(blocks, "mem", axis=1, tiled=True)
    count = shard_piece.shape[1]
    for offset in range(count):
        chosen = lax.dynamic_index_in_dim(block_cols, offset, 1, keepdims=False)
        picked = jnp.take(source, chosen, axis=0)
        tile_set = shard_piece[:, offset].astype(jnp.float32)
        summed = summed + jnp.einsum(
            "ipq,iqc->ipc", tile_set, picked, precision=lax.Precision.HIGHEST
        )
    horizontal = summed
    summed = empty
    shard_piece = lax.all_gather(blocks, "mem", axis=1, tiled=True)
    count = shard_piece.shape[1]
    for offset in range(count):
        owners = lax.dynamic_index_in_dim(inverse, offset, 1, keepdims=False)
        tile_set = shard_piece[:, offset].astype(jnp.float32)
        product = jnp.einsum("ipq,ipc->iqc", tile_set, horizontal, precision=lax.Precision.HIGHEST)
        summed = summed + jnp.take(product, owners, axis=0)
    level_groups = lax.axis_size("lev")
    arranged = summed.reshape(1, nodes_all, columns)
    transposed = lax.all_to_all(arranged, "lev", split_axis=1, concat_axis=0, tiled=True)
    owned_nodes = transposed.shape[1]
    split_levels = transposed.reshape(level_groups, owned_nodes, mem_dev, lev_dev)
    vertical_split = vertical.reshape(vertical.shape[0], level_groups, lev_dev)
    vertical_applied = jnp.einsum(
        "snkm,lsm->nkl", split_levels, vertical_split, precision=lax.Precision.HIGHEST
    )
    members_all = mem_dev * lax.axis_size("mem")
    weighted = vertical_applied * (member_weights / math.sqrt(members_all - 1))[None, :, None]
    return lax.psum_scatter(
        jnp.sum(perturb.astype(jnp.float32) * weighted[:, :, None, :], axis=1),
        "mem",
        scatter_dimension=0,
        tiled=True,
    )


def solution(mesh):
    in_specs = (
        P(None, "mem", "lev"),
        P("lev", "mem", None, None),
        P("mem"),
        P(None, "mem", None, None),
        P(),
        P(),
    )
    out_specs = P(("lev", "mem"), None, None)
    return jax.shard_map(shards, mesh=mesh, in_specs=in_specs, out_specs=out_specs, check_vma=False)
```

profile of v0, /device:TPU:0, one launch (start us, length us, event | category | flops | bytes accessed | tf_op | source)
XLA Modules:
  0.0 441.6 jit_solution(11678037962666474546)
XLA Ops:
  7.3 4.6 %reshape.26 = f32[64,64,128]{1,0,2:T(8,128)} reshape(f32[4096,8,16]{0,2,1:T(8,128)} %param.8) | data formatting | bytes 4194304 | tf_op jit(solution)/shard_map/reshape | solution.py:13
  11.9 3.8 copy.64
  48.7 4.8 %scatter_custom_fusion = s32[1024]{0:T(1024)S(1)} fusion(s32[1024]{0:T(1024)S(1)} %reshape.290, s32[1024]{0:T(1024)S(1)} %reshape.292, s32[]{:T(128)} %constant.116.clone.1), kind=kCustom, calls=%fused_computation.219 | custom fusion | bytes 4100
  53.7 68.5 %all-gather.2.cloned.1.call-done = bf16[64,16,64,64]{3,2,0,1:T(8,128)(2,1)} async-done(((bf16[64,1,64,64]{3,2,0,1:T(8,128)(2,1)}), bf16[64,16,64,64]{3,2,0,1:T(8,128)(2,1)}) %all-gather.2.cloned.1.call-update) | async-done | bytes 8388624 | tf_op jit(solution)/shard_map/all_gather | solution.py:32
  132.0 4.7 %fusion.16 = f32[64,128,64]{1,2,0:T(8,128)} fusion(f32[64,64,128]{2,1,0:T(8,128)} %gather_fusion.7, pred[64]{0:T(512)(128)(4,1)S(1)} %get-tuple-element.114, bf16[64,16,64,64]{3,2,0,1:T(8,128)(2,1)} %all-gather.2.cloned.1.call-done), kind=kOutput, calls=%fused_computation.66 | convolution fusion | flops 403177472 | bytes 5242944 | tf_op jit(solution)/shard_map/ipq,iqc->ipc/dot_general | solution.py:27
  166.2 11.1 %add_add_fusion = f32[64,128,64]{1,2,0:T(8,128)S(1)} fusion(f32[64,128,64]{1,2,0:T(8,128)} %fusion, f32[64,128,64]{1,2,0:T(8,128)} %fusion.2, f32[64,128,64]{1,2,0:T(8,128)} %fusion.4, f32[64,128,64]{1,2,0:T(8,128)} %fusion.6, f32[64,128,64]{1,2,0:T(8,128)} %fusion.8, f32[64,128,64]{1,2,0:T(8,128)S(1)} %fusion.10, f32[64,128,64]{1,2,0:T(8,128)S(1)} %fusion.12, ...), kind=kOutput, calls=%fused_computation.82 | convolution fusion | flops 411041792 | bytes 36700224 | tf_op jit(solution)/shard_map/ipq,iqc->ipc/dot_general | solution.py:27
  177.4 4.2 convolution_bitcast_fusion.15
  185.2 4.0 convolution_bitcast_fusion.14
  192.8 4.0 convolution_bitcast_fusion.13
  196.8 3.7 gather_fusion.18
  200.4 4.0 convolution_bitcast_fusion.12
  204.4 3.7 gather_fusion.19
  208.1 4.0 convolution_bitcast_fusion.11
  212.0 3.6 gather_fusion.20
  215.7 3.9 convolution_bitcast_fusion.10
  223.2 3.9 convolution_bitcast_fusion.9
  230.7 3.9 convolution_bitcast_fusion.8
  238.2 4.4 convolution_bitcast_fusion.7
  246.2 3.9 convolution_bitcast_fusion.6
  253.7 4.0 convolution_bitcast_fusion.5
  261.3 3.9 convolution_bitcast_fusion.4
  268.9 3.9 convolution_bitcast_fusion.3
  276.4 3.9 convolution_bitcast_fusion.2
  283.9 4.0 convolution_bitcast_fusion.1
  291.5 4.2 convolution_bitcast_fusion
  295.7 3.8 gather_fusion.31
  299.4 12.2 %select_add_fusion = f32[64,64,128]{2,1,0:T(8,128)} fusion(f32[64,64,128]{2,1,0:T(8,128)} %gather_fusion.31, f32[64,64,128]{2,1,0:T(8,128)} %gather_fusion.30, f32[64,64,128]{2,1,0:T(8,128)} %gather_fusion.29, f32[64,64,128]{2,1,0:T(8,128)} %gather_fusion.28, f32[64,64,128]{2,1,0:T(8,128)} %gather_fusion.27, f32[64,64,128]{2,1,0:T(8,128)} %gather_fusion.26, ...), kind=kLoop, calls=%fused_computation.35 | loop fusion | flops 16252928 | bytes 35652608 | tf_op jit(solution)/shard_map/add | solution.py:38
  311.7 4.5 %all-to-all-start = ((f32[1,4096,128]{2,0,1:T(1,128)}), f32[1,4096,128]{2,0,1:T(1,128)S(1)}, u32[]{:S(2)}, u32[]{:S(2)}) async-start(f32[1,4096,128]{2,0,1:T(1,128)} %bitcast.263), calls=%async_computation | async-start | bytes 4194304 | tf_op jit(solution)/shard_map/all_to_all | solution.py:41
  316.4 31.7 %all-to-all-done = f32[1,4096,128]{2,0,1:T(1,128)S(1)} async-done(((f32[1,4096,128]{2,0,1:T(1,128)}), f32[1,4096,128]{2,0,1:T(1,128)S(1)}, u32[]{:S(2)}, u32[]{:S(2)}) %all-to-all-start) | async-done | bytes 2097184 | tf_op jit(solution)/shard_map/all_to_all | solution.py:41
  348.0 4.1 copy.98
  360.4 5.6 %multiply_reduce_fusion = f32[512,5,128]{2,1,0:T(8,128)} fusion(bf16[512,8,5,128]{3,1,2,0:T(8,128)(2,1)S(1)} %bitcast.266, f32[512,8,128]{2,1,0:T(8,128)S(1)} %copy.101), kind=kLoop, calls=%fused_computation.33 | loop fusion | flops 7536640 | bytes 8650752 | tf_op jit(solution)/shard_map/reduce_sum | solution.py:51
  366.0 67.1 %reduce-scatter.2.cloned.1.call-done = f32[32,5,128]{2,1,0:T(8,128)} async-done(((f32[512,5,128]{2,1,0:T(8,128)}), f32[32,5,128]{2,1,0:T(8,128)}) %reduce-scatter.2.cloned.1.call-update) | async-done | bytes 81936 | tf_op jit(solution)/shard_map/reduce_scatter | solution.py:50
  (125 shorter events, 126.4 us)
Async XLA Ops:
  6.5 115.6 %all-gather.2.cloned.1.call-start = ((), (), s32[]{:S(2)}) async-start(), calls=%async_computation.2 | async-start | bytes 17825792 | tf_op jit(solution)/shard_map/all_gather | solution.py:32
  11.9 3.8 copy-start.16
  46.2 2.0 copy-start.17
  46.2 2.1 copy-start.18
  53.6 71.9 %copy-start.3 = (f32[64,64,128]{2,1,0:T(8,128)S(1)}, f32[64,64,128]{2,1,0:T(8,128)}, u32[]{:S(2)}) copy-start(f32[64,64,128]{2,1,0:T(8,128)} %gather_fusion.9) | copy-start | bytes 6291460
  122.2 14.5 %copy-start = (bf16[64,16,64,64]{3,2,0,1:T(8,128)(2,1)S(1)}, bf16[64,16,64,64]{3,2,0,1:T(8,128)(2,1)}, u32[]{:S(2)}) copy-start(bf16[64,16,64,64]{3,2,0,1:T(8,128)(2,1)} %all-gather.2.cloned.1.call-done) | copy-start | bytes 25165828
  132.0 4.7 %copy-start.4 = (f32[64,64,128]{2,1,0:T(8,128)S(1)}, f32[64,64,128]{2,1,0:T(8,128)}, u32[]{:S(2)}) copy-start(f32[64,64,128]{2,1,0:T(8,128)} %gather_fusion.6) | copy-start | bytes 6291460
  136.7 2.6 copy-start.5
  139.3 2.6 copy-start.6
  142.0 2.6 copy-start.7
  144.6 2.7 copy-start.8
  147.3 2.9 copy-start.9
  150.2 2.7 copy-start.10
  152.8 2.7 copy-start.11
  155.5 2.7 copy-start.12
  158.2 2.7 copy-start.13
  160.9 2.7 copy-start.14
  163.6 2.6 copy-start.1
  295.7 3.8 copy-start.2
  311.7 4.6 %copy-start.15 = (f32[128,128]{1,0:T(8,128)S(1)}, f32[128,128]{1,0:T(8,128)}, u32[]{:S(2)}) copy-start(f32[128,128]{1,0:T(8,128)} %param.13) | copy-start | bytes 196612
  311.7 4.6 %copy-start.19 = (f32[8]{0:T(128)S(1)}, f32[8]{0:T(128)}, u32[]{:S(2)}) copy-start(f32[8]{0:T(128)} %param.10) | copy-start | bytes 100
  311.7 36.3 %all-to-all-start = ((f32[1,4096,128]{2,0,1:T(1,128)}), f32[1,4096,128]{2,0,1:T(1,128)S(1)}, u32[]{:S(2)}, u32[]{:S(2)}) async-start(f32[1,4096,128]{2,0,1:T(1,128)} %bitcast.263), calls=%async_computation | async-start | bytes 4194304 | tf_op jit(solution)/shard_map/all_to_all | solution.py:41
  316.2 116.9 %reduce-scatter.2.cloned.1.call-start = ((), (), s32[]{:S(2)}) async-start(), calls=%async_computation.3 | async-start | bytes 2228224 | tf_op jit(solution)/shard_map/reduce_scatter | solution.py:50
  352.1 8.2 %slice-start = ((s8[5242880]{0:T(1024)(128)(4,1)}), s8[4194304]{0:T(1024)(128)(4,1)S(1)}, s32[]{:S(2)}) async-start(s8[5242880]{0:T(1024)(128)(4,1)} %bitcast.265), calls=%async_computation.4 | async-start | bytes 8388608
  355.5 4.9 %slice-start.1 = ((s8[5242880]{0:T(1024)(128)(4,1)}), s8[1048576]{0:T(1024)(128)(4,1)S(1)}, s32[]{:S(2)}) async-start(s8[5242880]{0:T(1024)(128)(4,1)} %bitcast.265), calls=%async_computation.5 | async-start | bytes 2097152
Sparse Core Ops, SparseCore 0:
  9.8 112.3 all-gather.1
  366.1 66.8 reduce-scatter.1
where the time goes:
time: 448 us; the launch traced here: 442 us
  waiting for transfers between devices  168 us (38%)
  matrix products  123 us (27%)
  local copies, waits for them, and re-layouts  114 us (25%)
  other arithmetic  18.2 us (4%)
  between operations  13.9 us (3%)
  starting transfers between devices  4.52 us (1%)
    all_gather x1, waiting for transfers between devices, shards(): shard_piece = lax.all_gather(blocks, 'mem', axis=1, tiled=True)  68.5 us
    reduce_scatter x1, waiting for transfers between devices, shards(): lax.psum_scatter(jnp.sum(perturb.astype(jnp.float32) * weighted[:, :, Non...  67.1 us
    dot_general x16, matrix products, shards(): jnp.einsum('ipq,ipc->iqc', tile_set, horizontal, precision=lax.Precision....  64.1 us
    gather x16, local copies, waits for them, and re-layouts, shards(): summed = summed + jnp.take(product, owners, axis=0)  58 us
    dot_general x16, matrix products, shards(): jnp.einsum('ipq,iqc->ipc', tile_set, picked, precision=lax.Precision.HIGH...  55.1 us
    gather x16, local copies, waits for them, and re-layouts, shards(): picked = jnp.take(source, chosen, axis=0)  32.4 us
    all_to_all x1, waiting for transfers between devices, shards(): lax.all_to_all(arranged, 'lev', split_axis=1, concat_axis=0, tiled=True)  31.7 us
    add x1, other arithmetic, shards(): summed = summed + jnp.take(product, owners, axis=0)  12.2 us
  transfers between devices with their start and end apart: 3, of which 3 were waited for; matrix products, arithmetic and copies ran while one was open for 11% of the time, Pallas kernels for 0%

commit v1 on v0

--- a/solution.py
+++ b/solution.py
@@ -29,7 +29,14 @@
         )
     horizontal = summed
     summed = empty
-    shard_piece = lax.all_gather(blocks, "mem", axis=1, tiled=True)
+
+    def _push_node(u_in):
+        x_new = jnp.stack([u_in for _ in range(lax.axis_size("mem"))])
+        oldest = lax.all_to_all(x_new, "mem", 0, 0)
+        d_next = jnp.concatenate(oldest, axis=1)
+        return d_next
+
+    shard_piece = _push_node(blocks)
     count = shard_piece.shape[1]
     for offset in range(count):
         owners = lax.dynamic_index_in_dim(inverse, offset, 1, keepdims=False)

time: 448 us -> 514 us (1.15)
  local copies, waits for them, and re-layouts: 114 us -> 173 us
  matrix products: 123 us -> 106 us
  waiting for transfers between devices: 168 us -> 181 us
  starting transfers between devices: 4.52 us -> 13.2 us
    all_to_all x0 -> x1, waiting for transfers between devices: none -> 75.9 us  [_push_node(): oldest = lax.all_to_all(x_new, 'mem', 0, 0)]
    all_gather x1, waiting for transfers between devices: 68.5 us -> 4.44 us  [shards(): shard_piece = lax.all_gather(blocks, 'mem', axis=1, tiled=True)]
    unnamed x50 -> x61, local copies, waits for them, and re-layouts: 8.57 us -> 53.3 us
    dot_general x16, matrix products: 64.1 us -> 48.8 us  [shards(): jnp.einsum('ipq,ipc->iqc', tile_set, horizontal, precision=lax.Precision....]
    reshape x0 -> x1, local copies, waits for them, and re-layouts: none -> 15 us  [_push_node(): d_next = jnp.concatenate(oldest, axis=1)]
    all_to_all x0 -> x1, starting transfers between devices: none -> 8.34 us  [_push_node(): oldest = lax.all_to_all(x_new, 'mem', 0, 0)]
  transfers between devices with their start and end apart: 3 -> 4, of which waited for: 3 -> 4; matrix products, arithmetic and copies ran while one was open for 11% -> 21% of each run, Pallas kernels for 0% -> 0%
where the time goes in v1:
time: 514 us; the launch traced here: 506 us
  waiting for transfers between devices  181 us (35%)
  local copies, waits for them, and re-layouts  173 us (34%)
  matrix products  106 us (21%)
  other arithmetic  18.4 us (4%)
  between operations  14.2 us (3%)
  starting transfers between devices  13.2 us (3%)
    all_to_all x1, waiting for transfers between devices, _push_node(): oldest = lax.all_to_all(x_new, 'mem', 0, 0)  75.9 us
    reduce_scatter x1, waiting for transfers between devices, shards(): lax.psum_scatter(jnp.sum(perturb.astype(jnp.float32) * weighted[:, :, Non...  68.3 us
    gather x16, local copies, waits for them, and re-layouts, shards(): summed = summed + jnp.take(product, owners, axis=0)  56.5 us
    dot_general x16, matrix products, shards(): jnp.einsum('ipq,iqc->ipc', tile_set, picked, precision=lax.Precision.HIGH...  53.5 us
    unnamed x61, local copies, waits for them, and re-layouts  53.3 us
    dot_general x16, matrix products, shards(): jnp.einsum('ipq,ipc->iqc', tile_set, horizontal, precision=lax.Precision....  48.8 us
    gather x16, local copies, waits for them, and re-layouts, shards(): picked = jnp.take(source, chosen, axis=0)  32.6 us
    all_to_all x1, waiting for transfers between devices, shards(): lax.all_to_all(arranged, 'lev', split_axis=1, concat_axis=0, tiled=True)  31.7 us
  transfers between devices with their start and end apart: 4, of which 4 were waited for; matrix products, arithmetic and copies ran while one was open for 21% of the time, Pallas kernels for 0%

profile of v1, /device:TPU:0, one launch (start us, length us, event | category | flops | bytes accessed | tf_op | source)
XLA Modules:
  0.0 505.9 jit_solution(17651089940313222050)
XLA Ops:
  8.9 6.3 %broadcast_bitcast_fusion = bf16[16,1,64,64,64]{4,3,2,1,0:T(8,128)(2,1)} fusion(bf16[64,64,64]{1,2,0:T(8,128)(2,1)S(1)} %copy.51), kind=kLoop, calls=%fused_computation.303 | loop fusion | bytes 8912896
  15.2 19.8 %reshape.407 = bf16[16,2,131072]{2,1,0:T(2,128)(2,1)} reshape(bf16[16,1,64,64,64]{4,3,2,1,0:T(8,128)(2,1)} %broadcast_bitcast_fusion) | data formatting | bytes 16777216
  35.0 8.3 %all-to-all-start = ((bf16[16,2,131072]{2,1,0:T(2,128)(2,1)}), bf16[16,2,131072]{2,1,0:T(2,128)(2,1)}, u32[]{:S(2)}, u32[]{:S(2)}) async-start(bf16[16,2,131072]{2,1,0:T(2,128)(2,1)} %reshape.407), calls=%async_computation | async-start | bytes 16777216 | tf_op jit(solution)/shard_map/all_to_all | solution.py:35
  46.4 3.8 copy.34
  83.4 4.3 scatter_custom_fusion
  87.9 75.9 %all-to-all-done = bf16[16,2,131072]{2,1,0:T(2,128)(2,1)} async-done(((bf16[16,2,131072]{2,1,0:T(2,128)(2,1)}), bf16[16,2,131072]{2,1,0:T(2,128)(2,1)}, u32[]{:S(2)}, u32[]{:S(2)}) %all-to-all-start) | async-done | bytes 8388640 | tf_op jit(solution)/shard_map/all_to_all | solution.py:35
  163.8 19.3 %reshape.408 = bf16[16,1,64,64,64]{4,3,2,1,0:T(8,128)(2,1)} reshape(bf16[16,2,131072]{2,1,0:T(2,128)(2,1)} %all-to-all-done) | data formatting | bytes 16777216
  183.1 15.0 %bitcast_bitcast_fusion = bf16[64,16,64,64]{2,3,0,1:T(8,128)(2,1)} fusion(bf16[16,1,64,64,64]{4,3,2,1,0:T(8,128)(2,1)} %reshape.408), kind=kLoop, calls=%fused_computation.302 | loop fusion | bytes 16777216 | tf_op jit(solution)/shard_map/reshape | solution.py:36
  198.1 4.4 all-gather.2.cloned.1.call-done
  205.2 3.9 fusion.12
  245.6 10.6 %add_add_fusion = f32[64,128,64]{1,2,0:T(8,128)S(1)} fusion(f32[64,128,64]{1,2,0:T(8,128)} %fusion, f32[64,128,64]{1,2,0:T(8,128)} %fusion.2, f32[64,128,64]{1,2,0:T(8,128)} %fusion.4, f32[64,128,64]{1,2,0:T(8,128)} %fusion.6, f32[64,128,64]{1,2,0:T(8,128)} %fusion.8, f32[64,128,64]{1,2,0:T(8,128)S(1)} %fusion.10, f32[64,128,64]{1,2,0:T(8,128)S(1)} %fusion.12, ...), kind=kOutput, calls=%fused_computation.82 | convolution fusion | flops 411041792 | bytes 36700224 | tf_op jit(solution)/shard_map/ipq,iqc->ipc/dot_general | solution.py:27
  256.1 4.1 convolution_bitcast_fusion.15
  260.2 3.9 convolution_bitcast_fusion.14
  264.2 3.7 convolution_bitcast_fusion.13
  267.9 3.8 convolution_bitcast_fusion.12
  271.7 3.9 convolution_bitcast_fusion.11
  275.6 3.7 convolution_bitcast_fusion.10
  307.2 3.6 gather_fusion.17
  310.8 3.6 gather_fusion.18
  321.6 3.6 gather_fusion.21
  325.2 3.6 gather_fusion.22
  339.7 3.7 gather_fusion.26
  343.3 3.7 gather_fusion.27
  354.2 3.7 gather_fusion.30
  357.8 3.7 gather_fusion.31
  361.5 12.3 %select_add_fusion = f32[64,64,128]{2,1,0:T(8,128)} fusion(f32[64,64,128]{2,1,0:T(8,128)} %gather_fusion.31, f32[64,64,128]{2,1,0:T(8,128)} %gather_fusion.30, f32[64,64,128]{2,1,0:T(8,128)} %gather_fusion.29, f32[64,64,128]{2,1,0:T(8,128)} %gather_fusion.28, f32[64,64,128]{2,1,0:T(8,128)} %gather_fusion.27, f32[64,64,128]{2,1,0:T(8,128)} %gather_fusion.26, ...), kind=kLoop, calls=%fused_computation.35 | loop fusion | flops 16252928 | bytes 35652608 | tf_op jit(solution)/shard_map/add | solution.py:45
  373.8 4.8 all-to-all-start.1
  378.7 31.7 %all-to-all-done.1 = f32[1,4096,128]{2,0,1:T(1,128)S(1)} async-done(((f32[1,4096,128]{2,0,1:T(1,128)}), f32[1,4096,128]{2,0,1:T(1,128)S(1)}, u32[]{:S(2)}, u32[]{:S(2)}) %all-to-all-start.1) | async-done | bytes 2097184 | tf_op jit(solution)/shard_map/all_to_all | solution.py:48
  410.4 4.3 copy.54
  418.0 3.7 bitcast_multiply_fusion
  422.9 5.8 %multiply_reduce_fusion = f32[512,5,128]{2,1,0:T(8,128)} fusion(bf16[512,8,5,128]{3,1,2,0:T(8,128)(2,1)S(1)} %bitcast.311, f32[512,8,128]{2,1,0:T(8,128)S(1)} %copy.57), kind=kLoop, calls=%fused_computation.33 | loop fusion | flops 7536640 | bytes 8650752 | tf_op jit(solution)/shard_map/reduce_sum | solution.py:58
  428.8 68.3 %reduce-scatter.2.cloned.1.call-done = f32[32,5,128]{2,1,0:T(8,128)} async-done(((f32[512,5,128]{2,1,0:T(8,128)}), f32[32,5,128]{2,1,0:T(8,128)}) %reduce-scatter.2.cloned.1.call-update) | async-done | bytes 81936 | tf_op jit(solution)/shard_map/reduce_scatter | solution.py:57
  (141 shorter events, 136.8 us)
Async XLA Ops:
  6.5 196.0 %all-gather.2.cloned.1.call-start = ((), (), s32[]{:S(2)}) async-start(), calls=%async_computation.3 | async-start | bytes 17825792 | tf_op jit(solution)/shard_map/all_gather | solution.py:21
  35.0 8.4 %copy-start.14 = (f32[4096,8,16]{0,2,1:T(8,128)S(1)}, f32[4096,8,16]{0,2,1:T(8,128)}, u32[]{:S(2)}) copy-start(f32[4096,8,16]{0,2,1:T(8,128)} %param.8) | copy-start | bytes 6291460
  35.0 128.8 %all-to-all-start = ((bf16[16,2,131072]{2,1,0:T(2,128)(2,1)}), bf16[16,2,131072]{2,1,0:T(2,128)(2,1)}, u32[]{:S(2)}, u32[]{:S(2)}) async-start(bf16[16,2,131072]{2,1,0:T(2,128)(2,1)} %reshape.407), calls=%async_computation | async-start | bytes 16777216 | tf_op jit(solution)/shard_map/all_to_all | solution.py:35
  46.4 3.8 copy-start.16
  80.9 2.0 copy-start.17
  80.9 2.1 copy-start.18
  183.1 19.5 %copy-start.2 = (f32[64,64,128]{2,1,0:T(8,128)S(1)}, f32[64,64,128]{2,1,0:T(8,128)}, u32[]{:S(2)}) copy-start(f32[64,64,128]{2,1,0:T(8,128)} %gather_fusion.10) | copy-start | bytes 6291460
  202.5 13.2 %copy-start = (bf16[64,16,64,64]{3,2,0,1:T(8,128)(2,1)S(1)}, bf16[64,16,64,64]{3,2,0,1:T(8,128)(2,1)}, u32[]{:S(2)}) copy-start(bf16[64,16,64,64]{3,2,0,1:T(8,128)(2,1)} %all-gather.2.cloned.1.call-done) | copy-start | bytes 25165828
  212.4 3.4 copy-start.3
  215.7 2.7 copy-start.4
  218.4 2.7 copy-start.5
  221.1 2.7 copy-start.6
  223.8 2.7 copy-start.7
  226.4 3.1 copy-start.8
  229.5 2.7 copy-start.9
  232.2 2.7 copy-start.10
  234.9 2.7 copy-start.11
  237.6 2.7 copy-start.12
  240.3 2.6 copy-start.13
  242.9 2.7 copy-start.1
  256.1 23.2 %slice-start = ((s8[16777216]{0:T(1024)(128)(4,1)}), s8[4194304]{0:T(1024)(128)(4,1)S(1)}, s32[]{:S(2)}) async-start(s8[16777216]{0:T(1024)(128)(4,1)} %bitcast.306), calls=%async_computation.5 | async-start | bytes 8388608
  260.2 19.1 %slice-start.1 = ((s8[16777216]{0:T(1024)(128)(4,1)}), s8[4194304]{0:T(1024)(128)(4,1)S(1)}, s32[]{:S(2)}) async-start(s8[16777216]{0:T(1024)(128)(4,1)} %bitcast.306), calls=%async_computation.6 | async-start | bytes 8388608
  267.9 11.5 %slice-start.2 = ((s8[16777216]{0:T(1024)(128)(4,1)}), s8[4194304]{0:T(1024)(128)(4,1)S(1)}, s32[]{:S(2)}) async-start(s8[16777216]{0:T(1024)(128)(4,1)} %bitcast.306), calls=%async_computation.7 | async-start | bytes 8388608
  271.7 7.7 %slice-start.3 = ((s8[16777216]{0:T(1024)(128)(4,1)}), s8[4194304]{0:T(1024)(128)(4,1)S(1)}, s32[]{:S(2)}) async-start(s8[16777216]{0:T(1024)(128)(4,1)} %bitcast.306), calls=%async_computation.8 | async-start | bytes 8388608
  373.8 4.9 copy-start.15
  373.8 5.0 copy-start.19
  373.8 36.6 %all-to-all-start.1 = ((f32[1,4096,128]{2,0,1:T(1,128)}), f32[1,4096,128]{2,0,1:T(1,128)S(1)}, u32[]{:S(2)}, u32[]{:S(2)}) async-start(f32[1,4096,128]{2,0,1:T(1,128)} %bitcast.308), calls=%async_computation.1 | async-start | bytes 4194304 | tf_op jit(solution)/shard_map/all_to_all | solution.py:48
  378.6 118.5 %reduce-scatter.2.cloned.1.call-start = ((), (), s32[]{:S(2)}) async-start(), calls=%async_computation.4 | async-start | bytes 2228224 | tf_op jit(solution)/shard_map/reduce_scatter | solution.py:57
  410.4 12.5 %slice-start.4 = ((s8[5242880]{0:T(1024)(128)(4,1)}), s8[1048576]{0:T(1024)(128)(4,1)S(1)}, s32[]{:S(2)}) async-start(s8[5242880]{0:T(1024)(128)(4,1)} %bitcast.310), calls=%async_computation.9 | async-start | bytes 2097152
  418.0 4.9 slice-start.5
Sparse Core Ops, SparseCore 0:
  9.8 192.7 all-gather.1
  428.9 68.0 reduce-scatter.1
